TPU v7x, 256 devices: a whole 4x4x8 slice. The times are simulated.
256 devices in a mesh: seq: 64 (over x, z, core), head: 4 (over y).
Axes of the slice: x: 4, y: 4, z: 8, core: 2. Of those that a mesh axis runs over, the one named last changes fastest.
Arguments:
- queries: bfloat16 [32768, 4096], P('seq', 'head'), may hold values from -6 to 6
- key_input: bfloat16 [32768, 4096], P('seq', 'head'), may hold values from -6 to 6
- value_input: bfloat16 [32768, 4096], P('seq', 'head'), may hold values from -40 to 40
- gate_input: bfloat16 [32768, 4096], P('seq', 'head'), may hold values from -8 to 8
- kv_state: float32 [32, 128, 128], P('head'), may hold values from -512 to 512
- norm_gain: float32 [4096], replicated, may hold values from 0.25 to 1.75
- out_weight: bfloat16 [4096, 4096], P('head', 'seq'), may hold values from -0.09375 to 0.09375
Outputs:
- output: bfloat16 [32768, 4096], P(('seq', 'head'))
All inputs are finite; a program needn't handle non-finite values.
Results may differ from a plain program's by a relative error of at most 0.02.
Values may be sent and summed in bfloat16 or wider, within the bound.
A program may use at most 128 MiB of HBM per device.

v0:
```python
import jax
import jax.numpy as jnp
from jax import lax
from jax.sharding import PartitionSpec as P

DH = 128
BLOCK = 512
epsilon = 1e-05


def entering(value, axis, join, neutral):
    place = lax.axis_index(axis)
    gathered = lax.all_gather(value.astype(jnp.bfloat16), axis)
    state = jnp.zeros_like(value) + jnp.asarray(neutral, value.dtype)

    def one(turn, state):
        return join(state, lax.dynamic_index_in_dim(gathered, turn, 0, False).astype(value.dtype))

    return lax.fori_loop(0, place, one, state)


def add_states(earlier, later):
    return earlier + later


def gated_norm(attn_rows, gate_rows, gain_part, total_width, square_sum):
    attn_float = attn_rows.astype(jnp.float32)
    scale = lax.rsqrt(square_sum / total_width + epsilon)
    normed = attn_float * scale[:, None] * gain_part[None, :]
    return (normed * jax.nn.sigmoid(gate_rows.astype(jnp.float32))).astype(jnp.bfloat16)


def shards(queries, key_input, value_input, gate_input, kv_state, norm_gain, out_weight):
    tok_rows = queries.shape[0]
    local_width = queries.shape[1]
    local_heads = local_width // DH
    num_blocks = tok_rows // BLOCK
    block_shape = (num_blocks, BLOCK, local_heads, DH)
    q_blocks = queries.reshape(block_shape)
    k_blocks = key_input.reshape(block_shape)
    v_blocks = value_input.reshape(block_shape)
    block_states = jnp.einsum(
        "nthd,nthe->nhde", k_blocks, v_blocks, preferred_element_type=jnp.float32
    )
    own_total = jnp.sum(block_states, axis=0)
    prefix = entering(own_total, "seq", add_states, jnp.zeros_like(own_total))
    start_state = kv_state + prefix
    running = jnp.cumsum(block_states, axis=0) - block_states
    before = start_state[None] + running
    carried_part = jnp.einsum(
        "nthd,nhde->nthe", q_blocks.astype(jnp.float32), before, precision=lax.Precision.HIGHEST
    )
    scores = jnp.einsum("nthd,nshd->nhts", q_blocks, k_blocks, preferred_element_type=jnp.float32)
    causal = jnp.arange(BLOCK)[:, None] >= jnp.arange(BLOCK)[None, :]
    weights = jnp.where(causal[None, None], scores, 0.0).astype(jnp.bfloat16)
    inner_part = jnp.einsum(
        "nhts,nshe->nthe", weights, v_blocks, preferred_element_type=jnp.float32
    )
    attn = (carried_part + inner_part).astype(jnp.bfloat16).reshape(tok_rows, local_width)
    total_width = local_width * lax.axis_size("head")
    tok_attn, tok_gate = (
        lax.all_to_all(attn, "head", split_axis=0, concat_axis=1, tiled=True),
        lax.all_to_all(gate_input, "head", split_axis=0, concat_axis=1, tiled=True),
    )
    tok_float = tok_attn.astype(jnp.float32)
    normed = gated_norm(
        tok_attn, tok_gate, norm_gain, total_width, jnp.sum(tok_float * tok_float, axis=1)
    )
    hidden = lax.all_to_all(normed, "head", split_axis=1, concat_axis=0, tiled=True)
    terms = jnp.dot(
        hidden,
        lax.all_gather(out_weight, "seq", axis=1, tiled=True),
        preferred_element_type=jnp.float32,
    )
    return lax.psum_scatter(terms.astype(jnp.bfloat16), "head", scatter_dimension=0, tiled=True)


def solution(mesh):
    in_specs = (
        P("seq", "head"),
        P("seq", "head"),
        P("seq", "head"),
        P("seq", "head"),
        P("head", None, None),
        P(),
        P("head", "seq"),
    )
    out_specs = P(("seq", "head"), None)
    return jax.shard_map(shards, mesh=mesh, in_specs=in_specs, out_specs=out_specs, check_vma=False)
```

profile of v0, /device:TPU:1, one launch (start us, length us, event | category | flops | bytes accessed | tf_op | source)
XLA Modules:
  0.0 307.6 jit_solution(3969963221888918470)
XLA Ops:
  6.5 2.9 fusion.34
  9.4 0.0 all-gather.4.cloned.1.call-start
  9.5 0.7 all-gather.4.cloned.1.call-update
  10.2 0.1 iota_compare_fusion
  10.3 103.8 %all-gather.6.cloned.1.call-done = bf16[512,128,128]{2,1,0:T(8,128)(2,1)} async-done(((bf16[8,128,128]{2,1,0:T(8,128)(2,1)}), bf16[512,128,128]{2,1,0:T(8,128)(2,1)}) %all-gather.6.cloned.1.call-update) | async-done | bytes 16777232 | tf_op jit(solution)/shard_map/all_gather | solution.py:13
  114.1 1.2 while.10
  114.1 1.1 convert_add_fusion.2
  115.3 2.4 fusion.13
  117.7 4.8 %fusion.10 = bf16[1,512,8,128]{1,3,2,0:T(8,128)(2,1)S(1)} fusion(f32[8,128,512]{2,1,0:T(8,128)} %fusion.13, pred[512,512]{1,0:T(8,128)(4,1)S(1)} %iota_compare_fusion, bf16[512,1024]{1,0:T(8,128)(2,1)S(1)} %copy-done, bf16[512,1024]{1,0:T(8,128)(2,1)} %param.11, bf16[512,1024]{1,0:T(8,128)(2,1)} %param.10), kind=kOutput, calls=%fused_computation.15 | convolution fusion | flops 1078984704 | bytes 6553600 | tf_op jit(solution)/shard_map/nhts,nshe->nthe/dot_general | solution.py:56
  122.5 0.3 all_to_all.32
  122.8 1.1 copy.40
  123.9 4.0 %all-to-all-start = ((bf16[4,128,1024]{1,2,0:T(8,128)(2,1)}), bf16[4,128,1024]{1,2,0:T(8,128)(2,1)S(1)}, u32[]{:S(2)}, u32[]{:S(2)}) async-start(bf16[4,128,1024]{1,2,0:T(8,128)(2,1)} %copy.40), calls=%async_computation | async-start | bytes 2097152 | tf_op jit(solution)/shard_map/all_to_all | solution.py:62
  128.0 1.3 copy.41
  129.3 13.6 %all-to-all-done = bf16[4,128,1024]{1,2,0:T(8,128)(2,1)S(1)} async-done(((bf16[4,128,1024]{1,2,0:T(8,128)(2,1)}), bf16[4,128,1024]{1,2,0:T(8,128)(2,1)S(1)}, u32[]{:S(2)}, u32[]{:S(2)}) %all-to-all-start) | async-done | bytes 1048608 | tf_op jit(solution)/shard_map/all_to_all | solution.py:62
  142.8 3.5 %all-to-all-start.1 = ((bf16[4,128,1024]{1,2,0:T(8,128)(2,1)}), bf16[4,128,1024]{1,2,0:T(8,128)(2,1)S(1)}, u32[]{:S(2)}, u32[]{:S(2)}) async-start(bf16[4,128,1024]{1,2,0:T(8,128)(2,1)} %copy.41), calls=%async_computation.1 | async-start | bytes 2097152 | tf_op jit(solution)/shard_map/all_to_all | solution.py:63
  146.3 0.0 reduce-scatter.2.cloned.1.call-start
  146.4 0.6 fusion.5
  147.0 13.3 %all-to-all-done.1 = bf16[4,128,1024]{1,2,0:T(8,128)(2,1)S(1)} async-done(((bf16[4,128,1024]{1,2,0:T(8,128)(2,1)}), bf16[4,128,1024]{1,2,0:T(8,128)(2,1)S(1)}, u32[]{:S(2)}, u32[]{:S(2)}) %all-to-all-start.1) | async-done | bytes 1048608 | tf_op jit(solution)/shard_map/all_to_all | solution.py:63
  160.2 0.8 fusion.21
  161.0 15.2 %all_to_all.42 = bf16[128,4,1024]{0,2,1:T(8,128)(2,1)S(1)} all-to-all(bf16[128,4,1024]{0,2,1:T(8,128)(2,1)S(1)} %fusion.21), channel_id=1, replica_groups=mesh['seq'=64,'head'=4] {'head'}, dimensions={1} | all-to-all | bytes 2097152 | tf_op jit(solution)/shard_map/all_to_all | solution.py:69
  176.2 0.5 copy.42
  176.7 20.2 %all-gather.4.cloned.1.call-done = bf16[1024,4096]{0,1:T(8,128)(2,1)} async-done(((bf16[1024,64]{0,1:T(8,128)(2,1)}), bf16[1024,4096]{0,1:T(8,128)(2,1)}) %all-gather.4.cloned.1.call-update) | async-done | bytes 8388624 | tf_op jit(solution)/shard_map/all_gather | solution.py:72
  196.9 9.4 %convolution_convert_fusion = bf16[512,4096]{1,0:T(8,128)(2,1)} fusion(bf16[512,1024]{1,0:T(8,128)(2,1)S(1)} %bitcast.73, bf16[1024,4096]{0,1:T(8,128)(2,1)} %all-gather.4.cloned.1.call-done), kind=kOutput, calls=%fused_computation.2 | convolution fusion | flops 4297064448 | bytes 13631488 | tf_op jit(solution)/shard_map/dot_general | solution.py:70
  206.4 94.8 %reduce-scatter.2.cloned.1.call-done = bf16[128,4096]{1,0:T(8,128)(2,1)} async-done(((bf16[512,4096]{1,0:T(8,128)(2,1)}), bf16[128,4096]{1,0:T(8,128)(2,1)}) %reduce-scatter.2.cloned.1.call-update) | async-done | bytes 1048592 | tf_op jit(solution)/shard_map/reduce_scatter | solution.py:75
  (14 shorter events, 0.1 us)
Async XLA Ops:
  6.5 108.7 %copy-start = (bf16[512,1024]{1,0:T(8,128)(2,1)S(1)}, bf16[512,1024]{1,0:T(8,128)(2,1)}, u32[]{:S(2)}) copy-start(bf16[512,1024]{1,0:T(8,128)(2,1)} %param.9) | copy-start | bytes 3145732
  6.5 107.5 %all-gather.6.cloned.1.call-start = ((), (), s32[]{:S(2)}) async-start(), calls=%async_computation.6 | async-start | bytes 17039360 | tf_op jit(solution)/shard_map/all_gather | solution.py:13
  9.4 187.4 %all-gather.4.cloned.1.call-start = ((), (), s32[]{:S(2)}) async-start(), calls=%async_computation.4 | async-start | bytes 8519680 | tf_op jit(solution)/shard_map/all_gather | solution.py:72
  114.1 1.2 copy-start.2
  122.8 5.1 %copy-start.1 = (bf16[512,1024]{1,0:T(8,128)(2,1)S(1)}, bf16[512,1024]{1,0:T(8,128)(2,1)}, u32[]{:S(2)}) copy-start(bf16[512,1024]{1,0:T(8,128)(2,1)} %param.12) | copy-start | bytes 3145732
  123.9 18.9 %all-to-all-start = ((bf16[4,128,1024]{1,2,0:T(8,128)(2,1)}), bf16[4,128,1024]{1,2,0:T(8,128)(2,1)S(1)}, u32[]{:S(2)}, u32[]{:S(2)}) async-start(bf16[4,128,1024]{1,2,0:T(8,128)(2,1)} %copy.40), calls=%async_computation | async-start | bytes 2097152 | tf_op jit(solution)/shard_map/all_to_all | solution.py:62
  127.9 18.4 %copy-start.3 = (f32[4096]{0:T(1024)S(1)}, f32[4096]{0:T(1024)}, u32[]{:S(2)}) copy-start(f32[4096]{0:T(1024)} %param.14) | copy-start | bytes 49156
  142.8 17.4 %all-to-all-start.1 = ((bf16[4,128,1024]{1,2,0:T(8,128)(2,1)}), bf16[4,128,1024]{1,2,0:T(8,128)(2,1)S(1)}, u32[]{:S(2)}, u32[]{:S(2)}) async-start(bf16[4,128,1024]{1,2,0:T(8,128)(2,1)} %copy.41), calls=%async_computation.1 | async-start | bytes 2097152 | tf_op jit(solution)/shard_map/all_to_all | solution.py:63
  146.3 154.8 %reduce-scatter.2.cloned.1.call-start = ((), (), s32[]{:S(2)}) async-start(), calls=%async_computation.5 | async-start | bytes 5242880 | tf_op jit(solution)/shard_map/reduce_scatter | solution.py:75
Sparse Core Ops, SparseCore 0:
  10.1 103.8 all-gather.5
  116.8 79.9 all-gather.3
  206.5 94.5 reduce-scatter.1
where the time goes:
time: 310 us; the launch traced here: 308 us
  waiting for transfers between devices  246 us (79%)
  matrix products  19.5 us (6%)
  blocking collectives  15.2 us (5%)
  between operations  13.2 us (4%)
  starting transfers between devices  7.63 us (2%)
  local copies, waits for them, and re-layouts  3.29 us (1%)
    all_gather x1, waiting for transfers between devices, entering(): gathered = lax.all_gather(value.astype(jnp.bfloat16), axis)  104 us
    reduce_scatter x1, waiting for transfers between devices, shards(): lax.psum_scatter(terms.astype(jnp.bfloat16), 'head', scatter_dimension=0,...  94.8 us
    all_gather x1, waiting for transfers between devices, shards(): lax.all_gather(out_weight, 'seq', axis=1, tiled=True)  20.2 us
    all_to_all x1, blocking collectives, shards(): lax.all_to_all(normed, 'head', split_axis=1, concat_axis=0, tiled=True)  15.2 us
    all_to_all x1, waiting for transfers between devices, shards(): lax.all_to_all(attn, 'head', split_axis=0, concat_axis=1, tiled=True)  13.6 us
    all_to_all x1, waiting for transfers between devices, shards(): lax.all_to_all(gate_input, 'head', split_axis=0, concat_axis=1, tiled=True)  13.3 us
    dot_general x1, matrix products, shards(): jnp.dot(hidden, lax.all_gather(out_weight, 'seq', axis=1, tiled=True), pr...  9.44 us
  transfers between devices with their start and end apart: 5, of which 5 were waited for; matrix products, arithmetic and copies ran while one was open for 4% of the time, Pallas kernels for 0%

commit v1 on v0

--- a/solution.py
+++ b/solution.py
@@ -6,6 +6,15 @@
 DH = 128
 BLOCK = 512
 epsilon = 1e-05
+
+
+def map_figure(mine):
+    table = []
+    for _ in range(lax.axis_size("seq")):
+        table.append(mine)
+    return jnp.concatenate(
+        lax.all_to_all(jnp.stack(table), axis_name="seq", split_axis=0, concat_axis=0), 1
+    )
 
 
 def entering(value, axis, join, neutral):
@@ -67,11 +76,7 @@
         tok_attn, tok_gate, norm_gain, total_width, jnp.sum(tok_float * tok_float, axis=1)
     )
     hidden = lax.all_to_all(normed, "head", split_axis=1, concat_axis=0, tiled=True)
-    terms = jnp.dot(
-        hidden,
-        lax.all_gather(out_weight, "seq", axis=1, tiled=True),
-        preferred_element_type=jnp.float32,
-    )
+    terms = jnp.dot(hidden, map_figure(out_weight), preferred_element_type=jnp.float32)
     return lax.psum_scatter(terms.astype(jnp.bfloat16), "head", scatter_dimension=0, tiled=True)
 
 

time: 310 us -> 506 us (1.63)
  waiting for transfers between devices: 246 us -> 361 us
  starting transfers between devices: 7.63 us -> 84 us
    all_to_all x0 -> x1, waiting for transfers between devices: none -> 185 us  [map_figure(): lax.all_to_all(jnp.stack(table), axis_name='seq', split_axis=0, concat_ax...]
    all_to_all x0 -> x1, starting transfers between devices: none -> 76.5 us  [map_figure(): lax.all_to_all(jnp.stack(table), axis_name='seq', split_axis=0, concat_ax...]
    reduce_scatter x1, waiting for transfers between devices: 94.8 us -> 44.3 us  [shards(): lax.psum_scatter(terms.astype(jnp.bfloat16), 'head', scatter_dimension=0,...]
    all_gather x1 -> x0, waiting for transfers between devices: 20.2 us -> none  [shards(): lax.all_gather(out_weight, 'seq', axis=1, tiled=True)]
  transfers between devices with their start and end apart: 5 -> 5, of which waited for: 5 -> 5; matrix products, arithmetic and copies ran while one was open for 4% -> 0% of each run, Pallas kernels for 0% -> 0%
where the time goes in v1:
time: 506 us; the launch traced here: 503 us
  waiting for transfers between devices  361 us (71%)
  starting transfers between devices  84 us (17%)
  matrix products  19.6 us (4%)
  blocking collectives  15.1 us (3%)
  between operations  13.5 us (3%)
  local copies, waits for them, and re-layouts  7.6 us (2%)
    all_to_all x1, waiting for transfers between devices, map_figure(): lax.all_to_all(jnp.stack(table), axis_name='seq', split_axis=0, concat_ax...  185 us
    all_gather x1, waiting for transfers between devices, entering(): gathered = lax.all_gather(value.astype(jnp.bfloat16), axis)  105 us
    all_to_all x1, starting transfers between devices, map_figure(): lax.all_to_all(jnp.stack(table), axis_name='seq', split_axis=0, concat_ax...  76.5 us
    reduce_scatter x1, waiting for transfers between devices, shards(): lax.psum_scatter(terms.astype(jnp.bfloat16), 'head', scatter_dimension=0,...  44.3 us
    all_to_all x1, blocking collectives, shards(): lax.all_to_all(normed, 'head', split_axis=1, concat_axis=0, tiled=True)  15.1 us
    all_to_all x1, waiting for transfers between devices, shards(): lax.all_to_all(attn, 'head', split_axis=0, concat_axis=1, tiled=True)  13.6 us
    all_to_all x1, waiting for transfers between devices, shards(): lax.all_to_all(gate_input, 'head', split_axis=0, concat_axis=1, tiled=True)  13.3 us
  transfers between devices with their start and end apart: 5, of which 5 were waited for; matrix products, arithmetic and copies ran while one was open for 0% of the time, Pallas kernels for 0%

profile of v1, /device:TPU:1, one launch (start us, length us, event | category | flops | bytes accessed | tf_op | source)
XLA Modules:
  0.0 503.3 jit_solution(13012139485158124862)
XLA Ops:
  6.5 2.9 fusion.34
  9.4 0.1 iota_compare_fusion
  9.5 104.5 %all-gather.3.cloned.1.call-done = bf16[512,128,128]{2,1,0:T(8,128)(2,1)} async-done(((bf16[8,128,128]{2,1,0:T(8,128)(2,1)}), bf16[512,128,128]{2,1,0:T(8,128)(2,1)}) %all-gather.3.cloned.1.call-update) | async-done | bytes 16777232 | tf_op jit(solution)/shard_map/all_gather | solution.py:22
  114.1 1.2 while.10
  114.1 1.1 convert_add_fusion.2
  115.3 2.4 fusion.13
  117.7 4.8 fusion.10
  122.5 0.3 all_to_all.35
  122.8 1.1 copy.41
  123.9 4.0 all-to-all-start
  128.0 1.3 copy.42
  129.3 13.6 %all-to-all-done = bf16[4,128,1024]{1,2,0:T(8,128)(2,1)S(1)} async-done(((bf16[4,128,1024]{1,2,0:T(8,128)(2,1)}), bf16[4,128,1024]{1,2,0:T(8,128)(2,1)S(1)}, u32[]{:S(2)}, u32[]{:S(2)}) %all-to-all-start) | async-done | bytes 1048608 | tf_op jit(solution)/shard_map/all_to_all | solution.py:71
  142.8 3.5 all-to-all-start.1
  146.4 0.6 fusion.5
  146.9 13.3 %all-to-all-done.1 = bf16[4,128,1024]{1,2,0:T(8,128)(2,1)S(1)} async-done(((bf16[4,128,1024]{1,2,0:T(8,128)(2,1)}), bf16[4,128,1024]{1,2,0:T(8,128)(2,1)S(1)}, u32[]{:S(2)}, u32[]{:S(2)}) %all-to-all-start.1) | async-done | bytes 1048608 | tf_op jit(solution)/shard_map/all_to_all | solution.py:72
  160.2 0.8 fusion.21
  161.0 15.1 %all_to_all.47 = bf16[128,4,1024]{0,2,1:T(8,128)(2,1)S(1)} all-to-all(bf16[128,4,1024]{0,2,1:T(8,128)(2,1)S(1)} %fusion.21), channel_id=1, replica_groups=mesh['seq'=64,'head'=4] {'head'}, dimensions={1} | all-to-all | bytes 2097152 | tf_op jit(solution)/shard_map/all_to_all | solution.py:78
  176.2 4.3 stack.2
  180.5 76.5 %all-to-all-start.3 = ((bf16[64,1024,64]{1,2,0:T(8,128)(2,1)}), bf16[64,1024,64]{1,2,0:T(8,128)(2,1)}, u32[]{:S(2)}, u32[]{:S(2)}) async-start(bf16[64,1024,64]{1,2,0:T(8,128)(2,1)} %stack.2), calls=%async_computation.3 | async-start | bytes 16777216 | tf_op jit(solution)/shard_map/all_to_all | solution.py:16
  256.9 0.0 reduce-scatter.2.cloned.1.call-start
  257.0 0.5 copy.43
  257.5 185.2 %all-to-all-done.3 = bf16[64,1024,64]{1,2,0:T(8,128)(2,1)} async-done(((bf16[64,1024,64]{1,2,0:T(8,128)(2,1)}), bf16[64,1024,64]{1,2,0:T(8,128)(2,1)}, u32[]{:S(2)}, u32[]{:S(2)}) %all-to-all-start.3) | async-done | bytes 8388640 | tf_op jit(solution)/shard_map/all_to_all | solution.py:16
  442.7 9.5 %convolution_convert_fusion = bf16[512,4096]{1,0:T(8,128)(2,1)} fusion(bf16[512,1024]{1,0:T(8,128)(2,1)S(1)} %bitcast.76, bf16[1024,4096]{0,1:T(8,128)(2,1)} %bitcast.10), kind=kOutput, calls=%fused_computation.2 | convolution fusion | flops 4297064448 | bytes 13631488 | tf_op jit(solution)/shard_map/dot_general | solution.py:79
  452.2 44.3 %reduce-scatter.2.cloned.1.call-done = bf16[128,4096]{1,0:T(8,128)(2,1)} async-done(((bf16[512,4096]{1,0:T(8,128)(2,1)}), bf16[128,4096]{1,0:T(8,128)(2,1)}) %reduce-scatter.2.cloned.1.call-update) | async-done | bytes 1048592 | tf_op jit(solution)/shard_map/reduce_scatter | solution.py:80
  (16 shorter events, 0.1 us)
Async XLA Ops:
  6.5 108.7 %copy-start = (bf16[512,1024]{1,0:T(8,128)(2,1)S(1)}, bf16[512,1024]{1,0:T(8,128)(2,1)}, u32[]{:S(2)}) copy-start(bf16[512,1024]{1,0:T(8,128)(2,1)} %param.9) | copy-start | bytes 3145732
  6.5 107.5 %all-gather.3.cloned.1.call-start = ((), (), s32[]{:S(2)}) async-start(), calls=%async_computation.6 | async-start | bytes 17039360 | tf_op jit(solution)/shard_map/all_gather | solution.py:22
  114.1 1.2 copy-start.2
  122.8 5.1 %copy-start.1 = (bf16[512,1024]{1,0:T(8,128)(2,1)S(1)}, bf16[512,1024]{1,0:T(8,128)(2,1)}, u32[]{:S(2)}) copy-start(bf16[512,1024]{1,0:T(8,128)(2,1)} %param.12) | copy-start | bytes 3145732
  123.9 18.9 %all-to-all-start = ((bf16[4,128,1024]{1,2,0:T(8,128)(2,1)}), bf16[4,128,1024]{1,2,0:T(8,128)(2,1)S(1)}, u32[]{:S(2)}, u32[]{:S(2)}) async-start(bf16[4,128,1024]{1,2,0:T(8,128)(2,1)} %copy.41), calls=%async_computation | async-start | bytes 2097152 | tf_op jit(solution)/shard_map/all_to_all | solution.py:71
  127.9 18.4 %copy-start.4 = (f32[4096]{0:T(1024)S(1)}, f32[4096]{0:T(1024)}, u32[]{:S(2)}) copy-start(f32[4096]{0:T(1024)} %param.14) | copy-start | bytes 49156
  142.8 17.4 %all-to-all-start.1 = ((bf16[4,128,1024]{1,2,0:T(8,128)(2,1)}), bf16[4,128,1024]{1,2,0:T(8,128)(2,1)S(1)}, u32[]{:S(2)}, u32[]{:S(2)}) async-start(bf16[4,128,1024]{1,2,0:T(8,128)(2,1)} %copy.42), calls=%async_computation.1 | async-start | bytes 2097152 | tf_op jit(solution)/shard_map/all_to_all | solution.py:72
  146.9 29.2 %copy-start.3 = (bf16[1024,64]{0,1:T(8,128)(2,1)S(1)}, bf16[1024,64]{0,1:T(8,128)(2,1)}, u32[]{:S(2)}) copy-start(bf16[1024,64]{0,1:T(8,128)(2,1)} %param.15) | copy-start | bytes 393220
  180.5 262.2 %all-to-all-start.3 = ((bf16[64,1024,64]{1,2,0:T(8,128)(2,1)}), bf16[64,1024,64]{1,2,0:T(8,128)(2,1)}, u32[]{:S(2)}, u32[]{:S(2)}) async-start(bf16[64,1024,64]{1,2,0:T(8,128)(2,1)} %stack.2), calls=%async_computation.3 | async-start | bytes 16777216 | tf_op jit(solution)/shard_map/all_to_all | solution.py:16
  256.9 239.5 %reduce-scatter.2.cloned.1.call-start = ((), (), s32[]{:S(2)}) async-start(), calls=%async_computation.5 | async-start | bytes 5242880 | tf_op jit(solution)/shard_map/reduce_scatter | solution.py:80
Sparse Core Ops, SparseCore 0:
  10.1 103.8 all-gather.2
  452.3 44.1 reduce-scatter.1
